TPU v7x, 256 devices: a whole 4x4x8 slice. The times are simulated.
256 devices in a mesh: dp: 4 (over y), tensor: 16 (over x_hi, z), rep: 4 (over x_lo, core).
Axes of the slice: x: 4 (x_hi: 2, x_lo: 2; x = x_hi * 2 + x_lo), y: 4, z: 8, core: 2. Of those that a mesh axis runs over, the one named last changes fastest.
Arguments:
- resid: bfloat16 [512, 8192], P('dp', 'rep'), may hold values from -94 to 94
- norm_gain: float32 [8192], P('rep'), may hold values from 0.25 to 1.75
- gate_weight: bfloat16 [4, 2048, 14336], P('rep', 'dp', 'tensor'), may hold values from -0.0625 to 0.0625
- up_weight: bfloat16 [4, 2048, 14336], P('rep', 'dp', 'tensor'), may hold values from -0.0625 to 0.0625
- down_weight: bfloat16 [14336, 4, 2048], P('tensor', 'rep', 'dp'), may hold values from -0.046875 to 0.046875
- enc_weight: bfloat16 [8192, 65536], P('rep', ('dp', 'tensor')), may hold values from -0.0625 to 0.0625
- enc_bias: float32 [65536], P(('dp', 'tensor')), may hold values from -3 to 3
- dec_weight: bfloat16 [65536, 8192], P(('dp', 'tensor'), 'rep'), may hold values from -1 to 1
- dec_bias: float32 [8192], P('rep'), may hold values from -3 to 3
- latent_ids: int32 [512, 64], replicated, may hold values from 0 to 65535, as said below
Outputs:
- resid_out: bfloat16 [512, 8192], P(('dp', 'tensor'), 'rep')
- recon: bfloat16 [512, 8192], P(('dp', 'tensor'), 'rep')
- error_ratio: float32 [512], P(('dp', 'tensor'))
Inputs may be any that keep to these rules, and one draw needn't show every extreme that they name: `latent_ids`: each row names 64 distinct latents: 8 latents in each of 8 distinct blocks of 128 consecutive latents (block b holds latents b * 128 to b * 128 + 127).
All inputs are finite; a program needn't handle non-finite values.
Results may differ from a plain program's by a relative error of at most 0.009.
Values may be sent and summed in bfloat16 or wider, within the bound.
No kernel may reach another device: no remote copies, remote signals or barrier semaphores. Data moves between devices by JAX's collectives and lax.ppermute only.
A program may use at most 64 MiB of HBM per device.

v0:
```python
import jax
import jax.numpy as jnp
from jax import lax
from jax.sharding import PartitionSpec as P


def place_mask(latent_ids, length, slab_first, slab_width):
    slots = latent_ids - slab_first
    inside = (slots >= 0) & (slots < slab_width)
    local_slot = jnp.where(inside, slots, slab_width)
    row_number = lax.broadcasted_iota(jnp.int32, slots.shape, 0)
    return (
        jnp.zeros((length, slab_width), jnp.bool_).at[row_number, local_slot].set(True, mode="drop")
    )


def body(
    resid,
    norm_gain,
    gate_weight,
    up_weight,
    down_weight,
    enc_weight,
    enc_bias,
    dec_weight,
    dec_bias,
    latent_ids,
):
    tok_grp, width_rep = resid.shape
    n_tensor = lax.axis_size("tensor")
    n_rep = lax.axis_size("rep")
    resid_f = resid.astype(jnp.float32)
    squares = lax.psum(jnp.sum(resid_f * resid_f, axis=1), "rep")
    inverse_rms = lax.rsqrt(squares / (width_rep * n_rep) + 1e-05)
    normed = (resid_f * inverse_rms[:, None] * norm_gain[None, :]).astype(jnp.bfloat16)
    gate_part = jnp.dot(
        normed,
        lax.all_gather(gate_weight, "dp", axis=1, tiled=True)[0],
        preferred_element_type=jnp.float32,
    )
    up_part = jnp.dot(
        normed,
        lax.all_gather(up_weight, "dp", axis=1, tiled=True)[0],
        preferred_element_type=jnp.float32,
    )
    gate_pre, up_pre = lax.psum((gate_part, up_part), "rep")
    hidden = (jax.nn.silu(gate_pre) * up_pre).astype(jnp.bfloat16)
    down_terms = jnp.dot(
        hidden,
        lax.all_gather(down_weight, "dp", axis=2, tiled=True)[:, 0, :],
        preferred_element_type=jnp.float32,
    )
    rows_dev = tok_grp // n_tensor
    block_sum = lax.psum(down_terms, "tensor")
    group_out = (resid_f + block_sum).astype(jnp.bfloat16)
    resid_rows = lax.dynamic_slice_in_dim(
        group_out, lax.axis_index("tensor") * rows_dev, rows_dev, 0
    )
    slab_input = lax.all_gather(group_out, "dp", axis=0, tiled=True)
    slab_width = enc_weight.shape[1]
    centred = (slab_input.astype(jnp.float32) - dec_bias[None, :]).astype(jnp.bfloat16)
    slab_first = (lax.axis_index("dp") * n_tensor + lax.axis_index("tensor")) * slab_width
    preact = lax.psum(jnp.dot(centred, enc_weight, preferred_element_type=jnp.float32), "rep")
    length = preact.shape[0]
    chosen = place_mask(latent_ids, length, slab_first, slab_width)
    actives = jnp.where(chosen, jnp.maximum(preact + enc_bias[None, :], 0.0), 0.0).astype(
        jnp.bfloat16
    )
    decoded = (
        lax.psum_scatter(
            jnp.dot(actives, dec_weight, preferred_element_type=jnp.float32),
            ("dp", "tensor"),
            scatter_dimension=0,
            tiled=True,
        )
        + dec_bias[None, :]
    )
    kept_f = resid_rows.astype(jnp.float32)
    misfit = kept_f - decoded
    miss_sum, energy = lax.psum(
        (jnp.sum(misfit * misfit, axis=1), jnp.sum(kept_f * kept_f, axis=1)), "rep"
    )
    error_ratio = miss_sum / (energy + 1e-06)
    return (resid_rows, decoded.astype(jnp.bfloat16), error_ratio)


def solution(mesh):
    in_specs = (
        P("dp", "rep"),
        P("rep"),
        P("rep", "dp", "tensor"),
        P("rep", "dp", "tensor"),
        P("tensor", "rep", "dp"),
        P("rep", ("dp", "tensor")),
        P(("dp", "tensor")),
        P(("dp", "tensor"), "rep"),
        P("rep"),
        P(),
    )
    out_specs = (P(("dp", "tensor"), "rep"), P(("dp", "tensor"), "rep"), P(("dp", "tensor")))
    return jax.shard_map(body, mesh=mesh, in_specs=in_specs, out_specs=out_specs, check_vma=False)
```

profile of v0, /device:TPU:1, one launch (start us, length us, event | category | flops | bytes accessed | tf_op | source)
XLA Modules:
  0.0 939.6 jit_solution(7741894260135573512)
XLA Ops:
  7.2 0.7 all-gather.7.cloned.1.call-update
  8.0 0.7 all-gather.5.cloned.1.call-update
  8.7 0.7 all-gather.9.cloned.1.call-update
  9.5 1.2 fusion.8
  10.7 8.3 psum.49
  18.9 41.2 %all-gather.7.cloned.1.call-done = bf16[1,2048,896]{2,1,0:T(8,128)(2,1)} async-done(((bf16[1,512,896]{2,1,0:T(8,128)(2,1)}), bf16[1,2048,896]{2,1,0:T(8,128)(2,1)}) %all-gather.7.cloned.1.call-update) | async-done | bytes 3670032 | tf_op jit(solution)/shard_map/all_gather | solution.py:43
  60.1 3.8 fusion.2
  63.9 44.8 %all-gather.5.cloned.1.call-done = bf16[1,2048,896]{2,1,0:T(8,128)(2,1)} async-done(((bf16[1,512,896]{2,1,0:T(8,128)(2,1)}), bf16[1,2048,896]{2,1,0:T(8,128)(2,1)}) %all-gather.5.cloned.1.call-update) | async-done | bytes 3670032 | tf_op jit(solution)/shard_map/all_gather | solution.py:38
  108.7 3.6 fusion.4
  112.4 44.9 %all-gather.9.cloned.1.call-done = bf16[896,1,2048]{2,0,1:T(8,128)(2,1)} async-done(((bf16[896,1,512]{2,0,1:T(8,128)(2,1)}), bf16[896,1,2048]{2,0,1:T(8,128)(2,1)}) %all-gather.9.cloned.1.call-update) | async-done | bytes 3670032 | tf_op jit(solution)/shard_map/all_gather | solution.py:50
  157.3 48.5 %all-reduce.10.cloned.1.call-done = (f32[128,896]{1,0:T(8,128)}, f32[128,896]{1,0:T(8,128)}) async-done(((f32[128,896]{1,0:T(8,128)}, f32[128,896]{1,0:T(8,128)}), (f32[128,896]{1,0:T(8,128)}, f32[128,896]{1,0:T(8,128)})) %all-reduce.10.cloned.1.call-update) | async-done | bytes 917520 | tf_op jit(solution)/shard_map/psum | solution.py:46
  205.8 4.0 fusion
  210.0 149.3 %all-reduce.6.cloned.1.call-done = f32[128,2048]{1,0:T(8,128)} async-done(((f32[128,2048]{1,0:T(8,128)}), f32[128,2048]{1,0:T(8,128)}) %all-reduce.6.cloned.1.call-update) | async-done | bytes 1048592 | tf_op jit(solution)/shard_map/psum | solution.py:54
  359.2 2.1 fusion.11
  361.5 41.0 %all-gather.11.cloned.1.call-done = bf16[512,2048]{1,0:T(8,128)(2,1)} async-done(((bf16[128,2048]{1,0:T(8,128)(2,1)}), bf16[512,2048]{1,0:T(8,128)(2,1)}) %all-gather.11.cloned.1.call-update) | async-done | bytes 2097168 | tf_op jit(solution)/shard_map/all_gather | solution.py:59
  402.4 6.5 fusion.6
  409.4 0.1 copy.13
  409.6 137.1 %scatter_custom_fusion = pred[524288]{0:T(1024)(128)(4,1)S(1)} fusion(s32[32768]{0:T(1024)S(1)} %reshape.26, pred[32768]{0:T(1024)(128)(4,1)S(1)} %broadcast.49, pred[]{:T(512)} %constant.14.clone.1), kind=kCustom, calls=%fused_computation.21 | custom fusion | bytes 524289
  546.7 0.6 reshape.25
  547.4 7.1 fusion.12
  554.5 321.2 %reduce-scatter.2.cloned.1.call-done = f32[8,2048]{1,0:T(8,128)} async-done(((f32[512,2048]{1,0:T(8,128)}), f32[8,2048]{1,0:T(8,128)}) %reduce-scatter.2.cloned.1.call-update) | async-done | bytes 65552 | tf_op jit(solution)/shard_map/reduce_scatter | solution.py:70
  875.7 1.6 fusion.23
  877.3 54.9 %all-reduce = (f32[8]{0:T(128)S(1)}, f32[8]{0:T(128)S(1)}) all-reduce(f32[8]{0:T(128)S(1)} %get-tuple-element.4, f32[8]{0:T(128)S(1)} %get-tuple-element.3), channel_id=1, replica_groups=mesh['dp'=4,'tensor'=16,'rep'=4] {'rep'}, use_global_device_ids=true, to_apply=%region_9.10 | all-reduce | flops 16 | bytes 128 | tf_op jit(solution)/shard_map/psum | solution.py:80
  932.2 0.5 add_divide_fusion
  (36 shorter events, 0.9 us)
Async XLA Ops:
  7.2 53.0 %all-gather.7.cloned.1.call-start = ((), (), s32[]{:S(2)}) async-start(), calls=%async_computation.2 | async-start | bytes 4587520 | tf_op jit(solution)/shard_map/all_gather | solution.py:43
  7.9 100.8 %copy-start = (bf16[128,2048]{1,0:T(8,128)(2,1)S(1)}, bf16[128,2048]{1,0:T(8,128)(2,1)}, u32[]{:S(2)}) copy-start(bf16[128,2048]{1,0:T(8,128)(2,1)} %param.10) | copy-start | bytes 1572868
  7.9 100.8 %copy-start.2 = (f32[2048]{0:T(1024)S(1)}, f32[2048]{0:T(1024)}, u32[]{:S(2)}) copy-start(f32[2048]{0:T(1024)} %param.11) | copy-start | bytes 24580
  7.9 100.8 %all-gather.5.cloned.1.call-start = ((), (), s32[]{:S(2)}) async-start(), calls=%async_computation.1 | async-start | bytes 4587520 | tf_op jit(solution)/shard_map/all_gather | solution.py:38
  8.7 148.6 %all-gather.9.cloned.1.call-start = ((), (), s32[]{:S(2)}) async-start(), calls=%async_computation.3 | async-start | bytes 4587520 | tf_op jit(solution)/shard_map/all_gather | solution.py:50
  9.4 196.4 %all-reduce.10.cloned.1.call-start = ((), (), s32[]{:S(2)}) async-start(), calls=%async_computation.8 | async-start | bytes 1835008 | tf_op jit(solution)/shard_map/psum | solution.py:46
  112.3 246.9 %all-reduce.6.cloned.1.call-start = ((), (), s32[]{:S(2)}) async-start(), calls=%async_computation.4 | async-start | bytes 2097152 | tf_op jit(solution)/shard_map/psum | solution.py:54
  205.8 196.6 %copy-start.3 = (f32[2048]{0:T(1024)S(1)}, f32[2048]{0:T(1024)}, u32[]{:S(2)}) copy-start(f32[2048]{0:T(1024)} %param.18) | copy-start | bytes 24580
  209.9 192.5 %all-gather.11.cloned.1.call-start = ((), (), s32[]{:S(2)}) async-start(), calls=%async_computation.5 | async-start | bytes 2621440 | tf_op jit(solution)/shard_map/all_gather | solution.py:59
  361.4 47.7 %copy-start.1 = (s32[512,64]{0,1:T(8,128)S(1)}, s32[512,64]{0,1:T(8,128)}, u32[]{:S(2)}) copy-start(s32[512,64]{0,1:T(8,128)} %param.19) | copy-start | bytes 393220
  361.4 47.7 %copy-start.5 = (s32[2]{0:T(128)S(1)}, s32[2]{0:T(128)}, u32[]{:S(2)}) copy-start(s32[2]{0:T(128)} %constant.46) | copy-start | bytes 28
  361.4 47.8 %copy-start.4 = (s32[2]{0:T(128)S(1)}, s32[2]{0:T(128)}, u32[]{:S(2)}) copy-start(s32[2]{0:T(128)} %constant.49) | copy-start | bytes 28
  361.4 185.9 %all-reduce.8.cloned.1.call-start = ((), (), s32[]{:S(2)}) async-start(), calls=%async_computation.6 | async-start | bytes 4194304 | tf_op jit(solution)/shard_map/psum | solution.py:63
  408.9 138.4 %copy-start.6 = (f32[1024]{0:T(1024)S(1)}, f32[1024]{0:T(1024)}, u32[]{:S(2)}) copy-start(f32[1024]{0:T(1024)} %param.16) | copy-start | bytes 12292
  409.0 466.7 %reduce-scatter.2.cloned.1.call-start = ((), (), s32[]{:S(2)}) async-start(), calls=%async_computation.7 | async-start | bytes 4259840 | tf_op jit(solution)/shard_map/reduce_scatter | solution.py:70
Sparse Core Ops, SparseCore 0:
  9.8 50.2 all-gather.6
  61.9 46.7 all-gather.4
  110.5 46.6 all-gather.8
  159.9 45.9 all-reduce.9
  210.0 149.1 all-reduce.5
  361.5 40.8 all-gather.10
  409.1 62.8 all-reduce.7
  554.6 320.9 reduce-scatter.1
where the time goes:
time: 940 us
  waiting for transfers between devices  693 us (74%)
  local copies, waits for them, and re-layouts  138 us (15%)
  blocking collectives  63.2 us (7%)
  matrix products  25 us (3%)
  between operations  14.3 us (2%)
    reduce_scatter x1, waiting for transfers between devices, body(): lax.psum_scatter(jnp.dot(actives, dec_weight, preferred_element_type=jnp....  321 us
    psum x1, waiting for transfers between devices, body(): block_sum = lax.psum(down_terms, 'tensor')  149 us
    unnamed x18, local copies, waits for them, and re-layouts  137 us
    psum x1, blocking collectives, body(): lax.psum((jnp.sum(misfit * misfit, axis=1), jnp.sum(kept_f * kept_f, axis...  54.9 us
    psum x1, waiting for transfers between devices, body(): gate_pre, up_pre = lax.psum((gate_part, up_part), 'rep')  48.5 us
    all_gather x1, waiting for transfers between devices, body(): lax.all_gather(down_weight, 'dp', axis=2, tiled=True)[:, 0, :]  44.9 us
    all_gather x1, waiting for transfers between devices, body(): lax.all_gather(gate_weight, 'dp', axis=1, tiled=True)[0]  44.8 us
    all_gather x1, waiting for transfers between devices, body(): lax.all_gather(up_weight, 'dp', axis=1, tiled=True)[0]  41.2 us
  transfers between devices with their start and end apart: 8, of which 7 were waited for; matrix products, arithmetic and copies ran while one was open for 16% of the time, Pallas kernels for 0%

commit v1 on v0

v1 whole, which is shorter than its diff:
```python
import jax
import jax.numpy as jnp
from jax import lax
from jax.experimental import pallas as pl
from jax.experimental.pallas import tpu as pltpu
from jax.sharding import Mesh, PartitionSpec as P

BF = jnp.bfloat16
F32 = jnp.float32
I32 = jnp.int32
VM = pl.BlockSpec(memory_space=pltpu.VMEM)
SM = pl.BlockSpec(memory_space=pltpu.SMEM)
ANY = pl.BlockSpec(memory_space=pltpu.HBM)
MIB = 1 << 20


def call(kernel, outs, n_in, scratch, flops, nbytes, limit=12, any_at=(), any_out=False):
    in_specs = [SM] + [ANY if i in any_at else VM for i in range(n_in)]
    return pl.pallas_call(
        kernel,
        out_shape=outs,
        in_specs=in_specs,
        out_specs=jax.tree.map(lambda _: ANY if any_out else VM, outs),
        scratch_shapes=scratch,
        compiler_params=pltpu.CompilerParams(vmem_limit_bytes=limit * MIB),
        cost_estimate=pl.CostEstimate(flops=flops, bytes_accessed=nbytes, transcendentals=0),
    )


def sds(shape, dt):
    return jax.ShapeDtypeStruct(shape, dt)


def mm(a, b):
    return jnp.dot(a, b, preferred_element_type=F32)


NC = 2
ROWS = 512 // NC
PER = 128 // NC


def gate_kernel(pos, p0, p1, p2, p3, gain, go, gp, *refs):
    outs, xsel, xg, pk, xr = refs[:4], refs[4], refs[5], refs[6], refs[7]
    for s, part in enumerate((p0, p1, p2, p3)):
        xr[s * 64:(s + 1) * 64, :] = part[...].astype(F32)
    xf = xr[...]
    xg[...] = (xf * gain[...]).astype(BF)
    ss = jnp.sum(xf * xf, axis=1, keepdims=True)
    hi = ss.astype(BF)
    lo = (ss - hi.astype(F32)).astype(BF)
    lane = lax.broadcasted_iota(I32, (256, 128), 1)
    tail = jnp.where(lane == 0, hi.astype(F32), jnp.where(lane == 1, lo.astype(F32), 0.0))
    pk[:, 896:] = tail.astype(BF)
    pk[:, :896] = (mm(xg[:, :512], go[...]) + mm(xg[:, 512:], gp[...])).astype(BF)
    for s in range(4):
        first = ((4 - s) % 4) * 64
        outs[s][...] = pk[first:first + 64, :]
    group = pos[3] // 4
    first = pl.multiple_of(lax.rem(pos[0] - group + 4, 4) * 64 + lax.rem(pos[3], 4) * 16, 16)
    xsel[...] = xr[pl.ds(first, 16), :]


def up_kernel(pos, xg, uo, up, *refs):
    outs, pk = refs[:4], refs[4]
    pk[...] = (mm(xg[:, :512], uo[...]) + mm(xg[:, 512:], up[...])).astype(BF)
    for s in range(4):
        first = ((4 - s) % 4) * 64
        outs[s][...] = pk[first:first + 64, :]


def down_kernel(pos, *refs):
    parts, down_own, down_oth, out, hid = refs[:4], refs[4], refs[5], refs[6], refs[7]
    for s in range(4):
        first = pl.multiple_of(lax.rem(pos[0] - s + 4, 4) * 64, 64)
        hid[pl.ds(first, 64), :] = parts[s][...]
    for q, w in enumerate((down_own, down_oth)):
        out[:, q * 512:(q + 1) * 512] = mm(hid[...], w[...]).astype(BF)


def split_kernel(pos, resid, mine, give):
    c = pos[2]
    for b in range(4):
        mine[b * 16:(b + 1) * 16, :] = resid[pl.ds(pl.multiple_of(b * 32 + c * 16, 16), 16), :]
        give[b * 16:(b + 1) * 16, :] = resid[pl.ds(pl.multiple_of(b * 32 + (1 - c) * 16, 16), 16), :]


def width_kernel(pos, mine, other, gain, gain_o, *outs):
    for s in range(4):
        col = pl.multiple_of(lax.rem(pos[0] + s, 4) * 512, 512)
        outs[s][:, :512] = mine[:, pl.ds(col, 512)]
        outs[s][:, 512:] = other[:, pl.ds(col, 512)]
    col = pl.multiple_of(pos[0] * 512, 512)
    outs[4][:, :512] = gain[:, pl.ds(col, 512)]
    outs[4][:, 512:] = gain_o[:, pl.ds(col, 512)]


def table_kernel(pos, sid, out):
    lane128 = lax.broadcasted_iota(I32, (32, 128), 1)
    block0 = pos[4] >> 7

    def step(t, carry):
        rows = pl.ds(pl.multiple_of(t * 32, 32), 32)
        ids = sid[rows, :]
        base = jnp.where(lax.rem(t, ROWS // 32) >= ROWS // 64, 64, 0)
        slots = []
        for s in range(8):
            acc = jnp.full((32, 128), -1, I32)
            for i in range(8):
                j = s * 8 + i
                acc = jnp.where((ids[:, j:j + 1] & 127) == lane128, base + j, acc)
            slots.append((jnp.broadcast_to((ids[:, s * 8:s * 8 + 1] >> 7) - block0, (32, 128)), acc))
        for b in range(8):
            acc = jnp.full((32, 128), -1, I32)
            for block, slot in slots:
                acc = jnp.where(block == b, slot, acc)
            out[rows, b * 128:(b + 1) * 128] = acc.astype(jnp.int8)
        return carry

    lax.fori_loop(0, 16, step, 0)


def lookup(values, index):
    return jnp.take_along_axis(values, index, axis=1, mode="promise_in_bounds")


def encode_kernel(pos, p0, p1, p2, p3, enc, bias, dec_bias, sidp, out, cent, pre):
    lane128 = lax.broadcasted_iota(I32, (64, 128), 1)
    for s, part in enumerate((p0, p1, p2, p3)):
        at = pl.ds(pl.multiple_of(lax.rem(pos[0] - s + 4, 4) * 512, 512), 512)
        cent[:, at] = (part[...].astype(F32) - dec_bias[:, at]).astype(BF)

    def product(n, carry):
        cols = pl.ds(pl.multiple_of(n * 256, 256), 256)
        pre[:, cols] = mm(cent[...], enc[:, cols]) + bias[:, cols]
        return carry

    lax.fori_loop(0, 4, product, 0)

    def compress(t, carry):
        rows = pl.ds(pl.multiple_of(t * 64, 64), 64)
        rows_hi = pl.ds(pl.multiple_of(ROWS // 2 + t * 64, 64), 64)
        ids = sidp[rows, :]
        lane = ids & 127
        block = (ids >> 7) - (pos[4] >> 7)
        acc = jnp.zeros((64, 128), F32)
        for b in range(8):
            lo = lookup(pre[rows, b * 128:(b + 1) * 128], lane)
            hi = lookup(pre[rows_hi, b * 128:(b + 1) * 128], lane)
            acc = jnp.where(block == b, jnp.where(lane128 < 64, lo, hi), acc)
        out[rows, :] = acc
        return carry

    lax.fori_loop(0, ROWS // 128, compress, 0)


def decode_kernel(pos, total, table, dec, *refs):
    outs, act, dense, y = refs[:4], refs[4], refs[5], refs[6]
    act[...] = jnp.maximum(total[...], 0.0)

    def step(t, carry):
        rows = pl.ds(pl.multiple_of(t * 64, 64), 64)
        vals = act[pl.ds(pl.multiple_of(lax.rem(t, ROWS // 128) * 64, 64), 64), :]
        for b in range(8):
            idx = table[rows, b * 128:(b + 1) * 128].astype(I32)
            got = lookup(vals, jnp.maximum(idx, 0))
            dense[rows, b * 128:(b + 1) * 128] = jnp.where(idx >= 0, got, 0.0).astype(BF)
        return carry

    lax.fori_loop(0, ROWS // 64, step, 0)

    def product(g, carry):
        at = pl.ds(pl.multiple_of(g * 256, 256), 256)
        y[:, at] = mm(dense[...], dec[:, at]).astype(BF)
        return carry

    lax.fori_loop(0, 8, product, 0)
    for s in range(4):
        first = pl.multiple_of(lax.rem(pos[0] + s, 4) * PER, PER)
        outs[s][...] = y[pl.ds(first, PER), :]


def swap(x, axis):
    return lax.ppermute(x, axis, [(0, 1), (1, 0)])


def dp_shift(x, s):
    return lax.ppermute(x, "dp", [(i, (i + s) % 4) for i in range(4)])


def body(resid, norm_gain, gate_w, up_w, down_w, enc, enc_bias, dec, dec_bias, ids):
    d, x, c = lax.axis_index("dp"), lax.axis_index("xlo"), lax.axis_index("core")
    h, z = lax.axis_index("xhi"), lax.axis_index("z")
    tensor = h * 8 + z
    pos = jnp.stack([d, x, c, tensor, (d * 16 + tensor) * 1024, d, d, d]).astype(I32)

    wide = norm_gain.reshape(1, 2048)
    mine, give = call(split_kernel, [sds((64, 2048), BF)] * 2, 1, [], 0, 1_000_000)(pos, resid)
    other, gain_o = swap(give, "core"), swap(wide, "core")
    gate, up, down = gate_w[0], up_w[0], down_w[:, 0, :]
    gate_o, up_o, down_o = swap(gate, "core"), swap(up, "core"), swap(down, "core")
    *xw, gain = call(
        width_kernel, [sds((64, 1024), BF)] * 4 + [sds((1, 1024), F32)], 4, [], 0, 1_000_000
    )(pos, mine, other, wide, gain_o)
    xs = [xw[0]] + [dp_shift(xw[s], s) for s in range(1, 4)]

    rank = jnp.sum((ids[:, :, None] < ids[:, None, :]).astype(I32), axis=1)
    place = lax.broadcasted_iota(I32, (1, 64, 64), 1)
    sid = jnp.sum(jnp.where(rank[:, None, :] == place, ids[:, None, :], 0), axis=2)
    sid = sid.reshape(4, NC, PER, 64).transpose(1, 0, 2, 3)
    sidp = sid.reshape(NC, 2, ROWS // 2, 64).transpose(0, 2, 1, 3).reshape(NC, ROWS // 2, 128)

    res = call(
        gate_kernel, [sds((64, 1024), BF)] * 4 + [sds((16, 1024), F32), sds((256, 1024), BF)], 7,
        [pltpu.VMEM((256, 1024), BF), pltpu.VMEM((256, 1024), F32)], 470_000_000, 3_000_000,
    )(pos, *xs, gain, gate, gate_o)
    xsel, xg = res[4], res[5]
    res_u = call(
        up_kernel, [sds((64, 896), BF)] * 4, 3, [pltpu.VMEM((256, 896), BF)], 470_000_000, 3_000_000
    )(pos, xg, up, up_o)

    def width_sum(pieces):
        tot = pieces[0].astype(F32)
        for s in range(1, 4):
            tot = tot + dp_shift(pieces[s], s).astype(F32)
        return tot + swap(tot.astype(BF), "xlo").astype(F32)

    tot_g, tot_u = width_sum(res[:4]), width_sum(res_u)
    inv = lax.rsqrt((tot_g[:, 896:897] + tot_g[:, 897:898]) / 8192 + 1e-05)
    hidden = (jax.nn.silu(tot_g[:, :896] * inv) * (tot_u * inv)).astype(BF)
    hid = [hidden] + [dp_shift(hidden, s) for s in range(1, 4)]
    terms = call(
        down_kernel, sds((256, 1024), BF), 6, [pltpu.VMEM((256, 896), BF)], 470_000_000, 3_000_000
    )(pos, *hid, down, down_o)
    terms = lax.all_to_all(terms, ("xhi", "z"), 0, 0, tiled=True)
    block_sum = jnp.sum(terms.reshape(16, 16, 1024).astype(F32), axis=0)
    rows = (xsel + block_sum).astype(BF)

    own, crossed = rows[:, :512], swap(rows[:, 512:], "core")
    rows = jnp.where(c == 0, jnp.stack([own, crossed]), jnp.stack([crossed, own])).reshape(32, 512)
    rows = jnp.broadcast_to(rows[None], (16, 32, 512)).reshape(512, 512)
    rows = lax.all_to_all(rows, ("xhi", "z"), 0, 0, tiled=True)
    rows = rows.reshape(4, NC, PER, 512)
    parts = []
    for k in range(NC):
        chunk = rows[:, k].reshape(ROWS, 512)
        if k:
            chunk, _ = lax.optimization_barrier((chunk, parts[-1]))
        parts.append([chunk] + [dp_shift(chunk, s) for s in range(1, 4)])

    at, _ = lax.optimization_barrier((pos, rows))
    table = call(table_kernel, sds((512, 1024), jnp.int8), 1, [], 1_000_000_000, 20_000_000)(
        at, sid.reshape(512, 64)
    )
    sidp, table = lax.optimization_barrier((sidp, table))

    chunk_of = tensor * 8 // PER
    first = d * PER + lax.rem(tensor * 8, PER)
    picks = [
        jnp.stack([lax.dynamic_slice_in_dim(p, first, 8, 0) for p in parts[k]]) for k in range(NC)
    ]
    rel = picks[0]
    for k in range(1, NC):
        rel = jnp.where(chunk_of == k, picks[k], rel)
    kept = jnp.concatenate(
        [lax.dynamic_index_in_dim(rel, (d - g + 4) % 4, 0, keepdims=False) for g in range(4)], 1
    )

    lead = ((x == 0) & (c == 0)).astype(F32)
    bias = (enc_bias * lead).reshape(1, 1024)
    wide_bias = dec_bias.reshape(1, 2048)
    pieces = []
    for k in range(NC):
        comp = call(
            encode_kernel, sds((ROWS // 2, 128), F32), 8,
            [pltpu.VMEM((ROWS, 2048), BF), pltpu.VMEM((ROWS, 1024), F32)],
            2_200_000_000 // NC, 6_000_000, limit=20,
        )(pos, *parts[k], enc, bias, wide_bias, sidp[k])
        for axis in ("core", "xlo"):
            comp = comp + swap(comp.astype(BF), axis).astype(F32)
        ys = call(
            decode_kernel, [sds((PER, 2048), BF)] * 4, 3,
            [pltpu.VMEM((ROWS // 2, 128), F32), pltpu.VMEM((ROWS, 1024), BF), pltpu.VMEM((ROWS, 2048), BF)],
            2_200_000_000 // NC, 8_000_000, limit=20,
        )(pos, comp, table[k * ROWS:(k + 1) * ROWS], dec)
        y = ys[0].astype(F32)
        for s in range(1, 4):
            y = y + dp_shift(ys[s], s).astype(F32)
        pieces.append(y.astype(BF))
    y = lax.all_to_all(jnp.concatenate(pieces, 0), ("xhi", "z"), 0, 0, tiled=True)
    decoded = jnp.sum(y.reshape(16, 8, 2048).astype(F32), axis=0) + wide_bias
    kept_f = kept.astype(F32)
    misfit = kept_f - decoded
    sums = jnp.stack([jnp.sum(misfit * misfit, axis=1), jnp.sum(kept_f * kept_f, axis=1)])
    for axis in ("core", "xlo"):
        sums = sums + swap(sums, axis)
    return kept, decoded.astype(BF), sums[0] / (sums[1] + 1e-06)


def solution(mesh):
    fine = Mesh(mesh.devices.reshape(4, 2, 8, 2, 2), ("dp", "xhi", "z", "xlo", "core"))
    rep, tensor, slabs = ("xlo", "core"), ("xhi", "z"), ("dp", "xhi", "z")
    in_specs = (
        P("dp", rep), P(rep), P(rep, "dp", tensor), P(rep, "dp", tensor), P(tensor, rep, "dp"),
        P(rep, slabs), P(slabs), P(slabs, rep), P(rep), P(),
    )
    out_specs = (P(slabs, rep), P(slabs, rep), P(slabs))
    return jax.shard_map(body, mesh=fine, in_specs=in_specs, out_specs=out_specs, check_vma=False)
```

time: 940 us -> 202 us (0.21)
  waiting for transfers between devices: 693 us -> 74.5 us
  local copies, waits for them, and re-layouts: 138 us -> 8.48 us
  starting transfers between devices: 0.32 us -> 59.2 us
  blocking collectives: 63.2 us -> 23.1 us
  Pallas kernels: 0 us -> 28.6 us
  matrix products: 25 us -> 0 us
  between operations: 14.3 us -> 1.2 us
    reduce_scatter x1 -> x0, waiting for transfers between devices: 321 us -> none  [body(): lax.psum_scatter(jnp.dot(actives, dec_weight, preferred_element_type=jnp....]
    psum x3 -> x0, waiting for transfers between devices: 198 us -> none  [the longest x1 149 us: body(): block_sum = lax.psum(down_terms, 'tensor')]
    all_gather x4 -> x0, waiting for transfers between devices: 172 us -> none  [the longest x1 44.9 us: body(): lax.all_gather(down_weight, 'dp', axis=2, tiled=True)[:, 0, :]]
    unnamed x18 -> x22, local copies, waits for them, and re-layouts: 137 us -> 6.32 us
    psum x2 -> x0, blocking collectives: 63.2 us -> none  [the longest x1 54.9 us: body(): lax.psum((jnp.sum(misfit * misfit, axis=1), jnp.sum(kept_f * kept_f, axis...]
    ppermute x0 -> x38, waiting for transfers between devices: none -> 47.9 us  [the longest x24 38.5 us: dp_shift(): return lax.ppermute(x, 'dp', [(i, (i + s) % 4) for i in range(4)])]
    ppermute x0 -> x38, starting transfers between devices: none -> 46.5 us  [the longest x24 27.7 us: dp_shift(): return lax.ppermute(x, 'dp', [(i, (i + s) % 4) for i in range(4)])]
    pallas_call x0 -> x10, Pallas kernels: none -> 28.6 us  [the longest x1 8.42 us: body(): call(table_kernel, sds((512, 1024), jnp.int8), 1, [], 1000000000, 20000000)]
  transfers between devices with their start and end apart: 8 -> 40, of which waited for: 7 -> 24; matrix products, arithmetic and copies ran while one was open for 16% -> 2% of each run, Pallas kernels for 0% -> 14%
where the time goes in v1:
time: 202 us; the launch traced here: 200 us
  waiting for transfers between devices  74.5 us (37%)
  starting transfers between devices  59.2 us (29%)
  Pallas kernels  28.6 us (14%)
  blocking collectives  23.1 us (11%)
  local copies, waits for them, and re-layouts  8.48 us (4%)
  other arithmetic  5.15 us (3%)
    ppermute x24, waiting for transfers between devices, dp_shift(): return lax.ppermute(x, 'dp', [(i, (i + s) % 4) for i in range(4)])  38.5 us
    ppermute x24, starting transfers between devices, dp_shift(): return lax.ppermute(x, 'dp', [(i, (i + s) % 4) for i in range(4)])  27.7 us
    all_to_all x1, blocking collectives, body(): terms = lax.all_to_all(terms, ('xhi', 'z'), 0, 0, tiled=True)  23.1 us
    ppermute x14, starting transfers between devices, swap(): return lax.ppermute(x, axis, [(0, 1), (1, 0)])  18.8 us
    all_to_all x1, waiting for transfers between devices, body(): lax.all_to_all(jnp.concatenate(pieces, 0), ('xhi', 'z'), 0, 0, tiled=True)  14.2 us
    all_to_all x1, waiting for transfers between devices, body(): rows = lax.all_to_all(rows, ('xhi', 'z'), 0, 0, tiled=True)  12.4 us
    ppermute x14, waiting for transfers between devices, swap(): return lax.ppermute(x, axis, [(0, 1), (1, 0)])  9.36 us
    pallas_call x1, Pallas kernels, body(): call(table_kernel, sds((512, 1024), jnp.int8), 1, [], 1000000000, 20000000)  8.42 us
  transfers between devices with their start and end apart: 40, of which 24 were waited for; matrix products, arithmetic and copies ran while one was open for 2% of the time, Pallas kernels for 14%

profile of v1, /device:TPU:1, one launch (start us, length us, event | category | flops | bytes accessed | tf_op | source)
XLA Modules:
  0.0 200.2 jit_solution(439990408980424173)
XLA Ops:
  0.6 3.3 %collective-permute-start.5 = (bf16[512,896]{1,0:T(8,128)(2,1)}, bf16[512,896]{1,0:T(8,128)(2,1)S(1)}, u32[]{:S(2)}, u32[]{:S(2)}) collective-permute-start(bf16[512,896]{1,0:T(8,128)(2,1)} %bitcast.74), channel_id=1, source_target_pairs={{0,1},{1,0},{2,3},{3,2},{4,5},{5,4},{6,7},{7,6},{8,9},{9,8},{10,11... | collective-permute-start | bytes 2752520 | tf_op jit(solution)/shard_map/ppermute | solution.py:184
  9.2 2.2 %collective-permute-start.3 = (bf16[64,1024]{1,0:T(8,128)(2,1)S(1)}, bf16[64,1024]{1,0:T(8,128)(2,1)S(1)}, u32[]{:S(2)}, u32[]{:S(2)}) collective-permute-start(bf16[64,1024]{1,0:T(8,128)(2,1)S(1)} %get-tuple-element.36), channel_id=1, source_target_pairs={{0,128},{64,192},{128,0},{192,64},{1,129},{65,193},{129,1},{193,65... | collective-permute-start | bytes 393224 | tf_op jit(solution)/shard_map/ppermute | solution.py:188
  12.5 3.3 %collective-permute-done.2.p1 = bf16[64,1024]{1,0:T(8,128)(2,1)S(1)} collective-permute-done((bf16[64,1024]{1,0:T(8,128)(2,1)S(1)}, bf16[64,1024]{1,0:T(8,128)(2,1)S(1)}, u32[]{:S(2)}, u32[]{:S(2)}) %collective-permute-start.2) | collective-permute-done | bytes 131104 | tf_op jit(solution)/shard_map/ppermute | solution.py:188
  22.3 3.1 %collective-permute-start.7 = (bf16[64,1024]{1,0:T(8,128)(2,1)S(1)}, bf16[64,1024]{1,0:T(8,128)(2,1)S(1)}, u32[]{:S(2)}, u32[]{:S(2)}) collective-permute-start(bf16[64,1024]{1,0:T(8,128)(2,1)S(1)} %get-tuple-element.42), channel_id=1, source_target_pairs={{0,128},{64,192},{128,0},{192,64},{1,129},{65,193},{129,1},{193,65... | collective-permute-start | bytes 393224 | tf_op jit(solution)/shard_map/ppermute | solution.py:188
  41.7 3.8 %collective-permute-start.17 = (bf16[64,896]{1,0:T(8,128)(2,1)S(1)}, bf16[64,896]{1,0:T(8,128)(2,1)S(1)}, u32[]{:S(2)}, u32[]{:S(2)}) collective-permute-start(bf16[64,896]{1,0:T(8,128)(2,1)S(1)} %multiply_convert_fusion.refs_0_), channel_id=1, source_target_pairs={{0,192},{64,0},{128,64},{192,128},{1,193},{65,1},{129,65},{193,129... | collective-permute-start | bytes 344072 | tf_op jit(solution)/shard_map/ppermute | solution.py:188
  47.8 2.8 %collective-permute-done.16.refs_2_ = bf16[64,896]{1,0:T(8,128)(2,1)S(1)} collective-permute-done((bf16[64,896]{1,0:T(8,128)(2,1)S(1)}, bf16[64,896]{1,0:T(8,128)(2,1)S(1)}, u32[]{:S(2)}, u32[]{:S(2)}) %collective-permute-start.16) | collective-permute-done | bytes 114720 | tf_op jit(solution)/shard_map/ppermute | solution.py:188
  53.6 23.1 %all_to_all.24 = bf16[16,16,1024]{2,1,0:T(8,128)(2,1)S(1)} all-to-all(bf16[16,16,1024]{2,1,0:T(8,128)(2,1)S(1)} %bitcast.61), channel_id=1, replica_groups=mesh['dp'=4,'xhi'=2,'z'=8,'xlo'=2,'core'=2] {'xhi','z'}, dimensions={0} | all-to-all | bytes 1048576 | tf_op jit(solution)/shard_map/all_to_all | solution.py:235
  76.8 4.5 %collective-permute-start.19 = (bf16[16,512]{1,0:T(8,128)(2,1)S(1)}, bf16[16,512]{1,0:T(8,128)(2,1)S(1)}, u32[]{:S(2)}, u32[]{:S(2)}) collective-permute-start(bf16[16,512]{1,0:T(8,128)(2,1)S(1)} %get-tuple-element.76), channel_id=1, source_target_pairs={{0,1},{1,0},{2,3},{3,2},{4,5},{5,4},{6,7},{7,6},{8,9},{9,8},{10,11... | collective-permute-start | bytes 49160 | tf_op jit(solution)/shard_map/ppermute | solution.py:184
  83.0 4.4 %all-to-all-start.1 = ((bf16[16,32,512]{2,1,0:T(8,128)(2,1)}), bf16[16,32,512]{2,1,0:T(8,128)(2,1)S(1)}, u32[]{:S(2)}, u32[]{:S(2)}) async-start(bf16[16,32,512]{2,1,0:T(8,128)(2,1)} %broadcast_in_dim.12), calls=%async_computation.1 | async-start | bytes 1048576 | tf_op jit(solution)/shard_map/all_to_all | solution.py:242
  90.2 12.4 %all-to-all-done.1 = bf16[16,32,512]{2,1,0:T(8,128)(2,1)S(1)} async-done(((bf16[16,32,512]{2,1,0:T(8,128)(2,1)}), bf16[16,32,512]{2,1,0:T(8,128)(2,1)S(1)}, u32[]{:S(2)}, u32[]{:S(2)}) %all-to-all-start.1) | async-done | bytes 524320 | tf_op jit(solution)/shard_map/all_to_all | solution.py:242
  105.0 8.4 %shard_map.126 = s8[512,1024]{1,0:T(32,128)(4,1)S(1)} custom-call(s32[8]{0:T(128)S(1)} %stack.79.pos, s32[512,64]{1,0:T(8,128)S(1)} %bitcast.78), custom_call_target="tpu_custom_call" | custom-call | flops 1000000000 | bytes 20000000 | tf_op jit(solution)/shard_map/pallas_call | solution.py:252
  113.9 3.7 %collective-permute-done.20.p1 = bf16[256,512]{1,0:T(8,128)(2,1)S(1)} collective-permute-done((bf16[256,512]{1,0:T(8,128)(2,1)S(1)}, bf16[256,512]{1,0:T(8,128)(2,1)S(1)}, u32[]{:S(2)}, u32[]{:S(2)}) %collective-permute-start.20) | collective-permute-done | bytes 262176 | tf_op jit(solution)/shard_map/ppermute | solution.py:188
  119.5 2.2 %copy-done = bf16[2048,1024]{1,0:T(8,128)(2,1)S(1)} copy-done((bf16[2048,1024]{1,0:T(8,128)(2,1)S(1)}, bf16[2048,1024]{1,0:T(8,128)(2,1)}, u32[]{:S(2)}) %copy-start) | copy-done | bytes 4194328
  121.7 3.4 %shard_map.127 = f32[128,128]{1,0:T(8,128)S(1)} custom-call(s32[8]{0:T(128)S(1)} %stack.79.pos, bf16[256,512]{1,0:T(8,128)(2,1)S(1)} %bitcast.70, bf16[256,512]{1,0:T(8,128)(2,1)S(1)} %collective-permute-done.20.p1, bf16[256,512]{1,0:T(8,128)(2,1)S(1)} %collective-permute-done.21.p2, bf16[256,512]{1,0:T(8,128)(2,1)S(1)} %collective-permute-done.22.p3, ...), custom_call_target="tpu_custom_call" | custom-call | flops 1100000000 | bytes 6000000 | tf_op jit(solution)/shard_map/pallas_call | solution.py:274
  125.1 2.9 %collective-permute-start.26 = (bf16[128,128]{1,0:T(8,128)(2,1)S(1)}, bf16[128,128]{1,0:T(8,128)(2,1)S(1)}, u32[]{:S(2)}, u32[]{:S(2)}) collective-permute-start(bf16[128,128]{1,0:T(8,128)(2,1)S(1)} %convert_element_type.131), channel_id=1, source_target_pairs={{0,1},{1,0},{2,3},{3,2},{4,5},{5,4},{6,7},{7,6},{8,9},{9,8},{10,11... | collective-permute-start | bytes 98312 | tf_op jit(solution)/shard_map/ppermute | solution.py:184
  129.3 3.6 %collective-permute-done.23.p1 = bf16[256,512]{1,0:T(8,128)(2,1)S(1)} collective-permute-done((bf16[256,512]{1,0:T(8,128)(2,1)S(1)}, bf16[256,512]{1,0:T(8,128)(2,1)S(1)}, u32[]{:S(2)}, u32[]{:S(2)}) %collective-permute-start.23) | collective-permute-done | bytes 262176 | tf_op jit(solution)/shard_map/ppermute | solution.py:188
  132.9 3.4 %shard_map.129 = f32[128,128]{1,0:T(8,128)S(1)} custom-call(s32[8]{0:T(128)S(1)} %stack.79.pos, bf16[256,512]{1,0:T(8,128)(2,1)S(1)} %bitcast.65, bf16[256,512]{1,0:T(8,128)(2,1)S(1)} %collective-permute-done.23.p1, bf16[256,512]{1,0:T(8,128)(2,1)S(1)} %collective-permute-done.24.p2, bf16[256,512]{1,0:T(8,128)(2,1)S(1)} %collective-permute-done.25.p3, ...), custom_call_target="tpu_custom_call" | custom-call | flops 1100000000 | bytes 6000000 | tf_op jit(solution)/shard_map/pallas_call | solution.py:274
  138.4 4.2 %shard_map.128 = (bf16[64,2048]{1,0:T(8,128)(2,1)S(1)}, bf16[64,2048]{1,0:T(8,128)(2,1)S(1)}, bf16[64,2048]{1,0:T(8,128)(2,1)S(1)}, bf16[64,2048]{1,0:T(8,128)(2,1)S(1)}) custom-call(s32[8]{0:T(128)S(1)} %stack.79.pos, f32[128,128]{1,0:T(8,128)S(1)} %convert_add_fusion.5.total, s8[256,1024]{1,0:T(32,128)(4,1)S(1)} %get-tuple-element.64.table, ...), custom_call_target="tpu_custom_call" | custom-call | flops 1100000000 | bytes 8000000 | tf_op jit(solution)/shard_map/pallas_call | solution.py:281
  145.6 4.2 %shard_map.130 = (bf16[64,2048]{1,0:T(8,128)(2,1)S(1)}, bf16[64,2048]{1,0:T(8,128)(2,1)S(1)}, bf16[64,2048]{1,0:T(8,128)(2,1)S(1)}, bf16[64,2048]{1,0:T(8,128)(2,1)S(1)}) custom-call(s32[8]{0:T(128)S(1)} %stack.79.pos, f32[128,128]{1,0:T(8,128)S(1)} %convert_add_fusion.3.total, s8[256,1024]{1,0:T(32,128)(4,1)S(1)} %get-tuple-element.65.table, ...), custom_call_target="tpu_custom_call" | custom-call | flops 1100000000 | bytes 8000000 | tf_op jit(solution)/shard_map/pallas_call | solution.py:281
  158.1 10.5 %collective-permute-done.33 = bf16[64,2048]{1,0:T(8,128)(2,1)S(1)} collective-permute-done((bf16[64,2048]{1,0:T(8,128)(2,1)S(1)}, bf16[64,2048]{1,0:T(8,128)(2,1)S(1)}, u32[]{:S(2)}, u32[]{:S(2)}) %collective-permute-start.33) | collective-permute-done | bytes 262176 | tf_op jit(solution)/shard_map/ppermute | solution.py:188
  169.5 8.3 %all-to-all-start.2 = ((bf16[16,8,2048]{2,1,0:T(8,128)(2,1)}), bf16[16,8,2048]{2,1,0:T(8,128)(2,1)S(1)}, u32[]{:S(2)}, u32[]{:S(2)}) async-start(bf16[16,8,2048]{2,1,0:T(8,128)(2,1)} %maximum_bitcast_fusion), calls=%async_computation.2 | async-start | bytes 1048576 | tf_op jit(solution)/shard_map/all_to_all | solution.py:290
  178.0 14.2 %all-to-all-done.2 = bf16[16,8,2048]{2,1,0:T(8,128)(2,1)S(1)} async-done(((bf16[16,8,2048]{2,1,0:T(8,128)(2,1)}), bf16[16,8,2048]{2,1,0:T(8,128)(2,1)S(1)}, u32[]{:S(2)}, u32[]{:S(2)}) %all-to-all-start.2) | async-done | bytes 524320 | tf_op jit(solution)/shard_map/all_to_all | solution.py:290
  193.1 3.2 %collective-permute-start.36 = (f32[2,8]{1,0:T(2,128)S(1)}, f32[2,8]{1,0:T(2,128)S(1)}, u32[]{:S(2)}, u32[]{:S(2)}) collective-permute-start(f32[2,8]{1,0:T(2,128)S(1)} %pad_maximum_fusion.1), channel_id=1, source_target_pairs={{0,1},{1,0},{2,3},{3,2},{4,5},{5,4},{6,7},{7,6},{8,9},{9,8},{10,11... | collective-permute-start | bytes 200 | tf_op jit(solution)/shard_map/ppermute | solution.py:184
  197.3 2.4 %collective-permute-done.37 = f32[2,8]{1,0:T(2,128)S(1)} collective-permute-done((f32[2,8]{1,0:T(2,128)S(1)}, f32[2,8]{1,0:T(2,128)S(1)}, u32[]{:S(2)}, u32[]{:S(2)}) %collective-permute-start.37) | collective-permute-done | bytes 96 | tf_op jit(solution)/shard_map/ppermute | solution.py:184
  (137 shorter events, 61.5 us)
Async XLA Ops:
  0.6 17.7 %collective-permute-start.5 = (bf16[512,896]{1,0:T(8,128)(2,1)}, bf16[512,896]{1,0:T(8,128)(2,1)S(1)}, u32[]{:S(2)}, u32[]{:S(2)}) collective-permute-start(bf16[512,896]{1,0:T(8,128)(2,1)} %bitcast.74), channel_id=1, source_target_pairs={{0,1},{1,0},{2,3},{3,2},{4,5},{5,4},{6,7},{7,6},{8,9},{9,8},{10,11... | collective-permute-start | bytes 2752520 | tf_op jit(solution)/shard_map/ppermute | solution.py:184
  4.0 22.5 %collective-permute-start.10 = (bf16[512,896]{1,0:T(8,128)(2,1)}, bf16[512,896]{1,0:T(8,128)(2,1)S(1)}, u32[]{:S(2)}, u32[]{:S(2)}) collective-permute-start(bf16[512,896]{1,0:T(8,128)(2,1)} %bitcast.72), channel_id=1, source_target_pairs={{0,1},{1,0},{2,3},{3,2},{4,5},{5,4},{6,7},{7,6},{8,9},{9,8},{10,11... | collective-permute-start | bytes 2752520 | tf_op jit(solution)/shard_map/ppermute | solution.py:184
  9.2 8.4 %collective-permute-start.3 = (bf16[64,1024]{1,0:T(8,128)(2,1)S(1)}, bf16[64,1024]{1,0:T(8,128)(2,1)S(1)}, u32[]{:S(2)}, u32[]{:S(2)}) collective-permute-start(bf16[64,1024]{1,0:T(8,128)(2,1)S(1)} %get-tuple-element.36), channel_id=1, source_target_pairs={{0,128},{64,192},{128,0},{192,64},{1,129},{65,193},{129,1},{193,65... | collective-permute-start | bytes 393224 | tf_op jit(solution)/shard_map/ppermute | solution.py:188
  11.4 6.9 %collective-permute-start.4 = (bf16[64,1024]{1,0:T(8,128)(2,1)S(1)}, bf16[64,1024]{1,0:T(8,128)(2,1)S(1)}, u32[]{:S(2)}, u32[]{:S(2)}) collective-permute-start(bf16[64,1024]{1,0:T(8,128)(2,1)S(1)} %get-tuple-element.37), channel_id=1, source_target_pairs={{0,192},{64,0},{128,64},{192,128},{1,193},{65,1},{129,65},{193,129... | collective-permute-start | bytes 393224 | tf_op jit(solution)/shard_map/ppermute | solution.py:188
  20.8 9.9 %collective-permute-start.6 = (bf16[64,1024]{1,0:T(8,128)(2,1)S(1)}, bf16[64,1024]{1,0:T(8,128)(2,1)S(1)}, u32[]{:S(2)}, u32[]{:S(2)}) collective-permute-start(bf16[64,1024]{1,0:T(8,128)(2,1)S(1)} %get-tuple-element.41), channel_id=1, source_target_pairs={{0,64},{64,128},{128,192},{192,0},{1,65},{65,129},{129,193},{193,1... | collective-permute-start | bytes 393224 | tf_op jit(solution)/shard_map/ppermute | solution.py:188
  22.3 9.0 %collective-permute-start.7 = (bf16[64,1024]{1,0:T(8,128)(2,1)S(1)}, bf16[64,1024]{1,0:T(8,128)(2,1)S(1)}, u32[]{:S(2)}, u32[]{:S(2)}) collective-permute-start(bf16[64,1024]{1,0:T(8,128)(2,1)S(1)} %get-tuple-element.42), channel_id=1, source_target_pairs={{0,128},{64,192},{128,0},{192,64},{1,129},{65,193},{129,1},{193,65... | collective-permute-start | bytes 393224 | tf_op jit(solution)/shard_map/ppermute | solution.py:188
  25.4 7.9 %collective-permute-start.8 = (bf16[64,1024]{1,0:T(8,128)(2,1)S(1)}, bf16[64,1024]{1,0:T(8,128)(2,1)S(1)}, u32[]{:S(2)}, u32[]{:S(2)}) collective-permute-start(bf16[64,1024]{1,0:T(8,128)(2,1)S(1)} %get-tuple-element.43), channel_id=1, source_target_pairs={{0,192},{64,0},{128,64},{192,128},{1,193},{65,1},{129,65},{193,129... | collective-permute-start | bytes 393224 | tf_op jit(solution)/shard_map/ppermute | solution.py:188
  25.4 20.8 %collective-permute-start.18 = (bf16[896,512]{1,0:T(8,128)(2,1)}, bf16[896,512]{1,0:T(8,128)(2,1)S(1)}, u32[]{:S(2)}, u32[]{:S(2)}) collective-permute-start(bf16[896,512]{1,0:T(8,128)(2,1)} %bitcast.76), channel_id=1, source_target_pairs={{0,1},{1,0},{2,3},{3,2},{4,5},{5,4},{6,7},{7,6},{8,9},{9,8},{10,11... | collective-permute-start | bytes 2752520 | tf_op jit(solution)/shard_map/ppermute | solution.py:184
  83.0 19.5 %all-to-all-start.1 = ((bf16[16,32,512]{2,1,0:T(8,128)(2,1)}), bf16[16,32,512]{2,1,0:T(8,128)(2,1)S(1)}, u32[]{:S(2)}, u32[]{:S(2)}) async-start(bf16[16,32,512]{2,1,0:T(8,128)(2,1)} %broadcast_in_dim.12), calls=%async_computation.1 | async-start | bytes 1048576 | tf_op jit(solution)/shard_map/all_to_all | solution.py:242
  102.6 11.3 %collective-permute-start.22 = (bf16[256,512]{1,0:T(8,128)(2,1)S(1)}, bf16[256,512]{1,0:T(8,128)(2,1)S(1)}, u32[]{:S(2)}, u32[]{:S(2)}) collective-permute-start(bf16[256,512]{1,0:T(8,128)(2,1)S(1)} %bitcast.67), channel_id=1, source_target_pairs={{0,192},{64,0},{128,64},{192,128},{1,193},{65,1},{129,65},{193,129... | collective-permute-start | bytes 786440 | tf_op jit(solution)/shard_map/ppermute | solution.py:188
  103.4 10.6 %collective-permute-start.21 = (bf16[256,512]{1,0:T(8,128)(2,1)S(1)}, bf16[256,512]{1,0:T(8,128)(2,1)S(1)}, u32[]{:S(2)}, u32[]{:S(2)}) collective-permute-start(bf16[256,512]{1,0:T(8,128)(2,1)S(1)} %bitcast.68), channel_id=1, source_target_pairs={{0,128},{64,192},{128,0},{192,64},{1,129},{65,193},{129,1},{193,65... | collective-permute-start | bytes 786440 | tf_op jit(solution)/shard_map/ppermute | solution.py:188
  104.2 13.4 %collective-permute-start.20 = (bf16[256,512]{1,0:T(8,128)(2,1)S(1)}, bf16[256,512]{1,0:T(8,128)(2,1)S(1)}, u32[]{:S(2)}, u32[]{:S(2)}) collective-permute-start(bf16[256,512]{1,0:T(8,128)(2,1)S(1)} %bitcast.69), channel_id=1, source_target_pairs={{0,64},{64,128},{128,192},{192,0},{1,65},{65,129},{129,193},{193,1... | collective-permute-start | bytes 786440 | tf_op jit(solution)/shard_map/ppermute | solution.py:188
  117.7 11.6 %collective-permute-start.25 = (bf16[256,512]{1,0:T(8,128)(2,1)S(1)}, bf16[256,512]{1,0:T(8,128)(2,1)S(1)}, u32[]{:S(2)}, u32[]{:S(2)}) collective-permute-start(bf16[256,512]{1,0:T(8,128)(2,1)S(1)} %bitcast.62), channel_id=1, source_target_pairs={{0,192},{64,0},{128,64},{192,128},{1,193},{65,1},{129,65},{193,129... | collective-permute-start | bytes 786440 | tf_op jit(solution)/shard_map/ppermute | solution.py:188
  117.7 11.6 %collective-permute-start.24 = (bf16[256,512]{1,0:T(8,128)(2,1)S(1)}, bf16[256,512]{1,0:T(8,128)(2,1)S(1)}, u32[]{:S(2)}, u32[]{:S(2)}) collective-permute-start(bf16[256,512]{1,0:T(8,128)(2,1)S(1)} %bitcast.63), channel_id=1, source_target_pairs={{0,128},{64,192},{128,0},{192,64},{1,129},{65,193},{129,1},{193,65... | collective-permute-start | bytes 786440 | tf_op jit(solution)/shard_map/ppermute | solution.py:188
  118.6 14.3 %collective-permute-start.23 = (bf16[256,512]{1,0:T(8,128)(2,1)S(1)}, bf16[256,512]{1,0:T(8,128)(2,1)S(1)}, u32[]{:S(2)}, u32[]{:S(2)}) collective-permute-start(bf16[256,512]{1,0:T(8,128)(2,1)S(1)} %bitcast.64), channel_id=1, source_target_pairs={{0,64},{64,128},{128,192},{192,0},{1,65},{65,129},{129,193},{193,1... | collective-permute-start | bytes 786440 | tf_op jit(solution)/shard_map/ppermute | solution.py:188
  128.9 8.2 %collective-permute-start.27 = (bf16[128,128]{1,0:T(8,128)(2,1)S(1)}, bf16[128,128]{1,0:T(8,128)(2,1)S(1)}, u32[]{:S(2)}, u32[]{:S(2)}) collective-permute-start(bf16[128,128]{1,0:T(8,128)(2,1)S(1)} %fusion.5), channel_id=1, source_target_pairs={{0,2},{2,0},{1,3},{3,1},{4,6},{6,4},{5,7},{7,5},{8,10},{10,8},{9,1... | collective-permute-start | bytes 98312 | tf_op jit(solution)/shard_map/ppermute | solution.py:184
  138.0 7.6 %collective-permute-start.32 = (bf16[128,128]{1,0:T(8,128)(2,1)S(1)}, bf16[128,128]{1,0:T(8,128)(2,1)S(1)}, u32[]{:S(2)}, u32[]{:S(2)}) collective-permute-start(bf16[128,128]{1,0:T(8,128)(2,1)S(1)} %fusion.6), channel_id=1, source_target_pairs={{0,2},{2,0},{1,3},{3,1},{4,6},{6,4},{5,7},{7,5},{8,10},{10,8},{9,1... | collective-permute-start | bytes 98312 | tf_op jit(solution)/shard_map/ppermute | solution.py:184
  142.5 9.5 %collective-permute-start.28 = (bf16[64,2048]{1,0:T(8,128)(2,1)S(1)}, bf16[64,2048]{1,0:T(8,128)(2,1)S(1)}, u32[]{:S(2)}, u32[]{:S(2)}) collective-permute-start(bf16[64,2048]{1,0:T(8,128)(2,1)S(1)} %get-tuple-element.54), channel_id=1, source_target_pairs={{0,64},{64,128},{128,192},{192,0},{1,65},{65,129},{129,193},{193,1... | collective-permute-start | bytes 786440 | tf_op jit(solution)/shard_map/ppermute | solution.py:188
  142.6 13.5 %collective-permute-start.29 = (bf16[64,2048]{1,0:T(8,128)(2,1)S(1)}, bf16[64,2048]{1,0:T(8,128)(2,1)S(1)}, u32[]{:S(2)}, u32[]{:S(2)}) collective-permute-start(bf16[64,2048]{1,0:T(8,128)(2,1)S(1)} %get-tuple-element.55), channel_id=1, source_target_pairs={{0,128},{64,192},{128,0},{192,64},{1,129},{65,193},{129,1},{193,65... | collective-permute-start | bytes 786440 | tf_op jit(solution)/shard_map/ppermute | solution.py:188
  144.7 13.3 %collective-permute-start.30 = (bf16[64,2048]{1,0:T(8,128)(2,1)S(1)}, bf16[64,2048]{1,0:T(8,128)(2,1)S(1)}, u32[]{:S(2)}, u32[]{:S(2)}) collective-permute-start(bf16[64,2048]{1,0:T(8,128)(2,1)S(1)} %get-tuple-element.56), channel_id=1, source_target_pairs={{0,192},{64,0},{128,64},{192,128},{1,193},{65,1},{129,65},{193,129... | collective-permute-start | bytes 786440 | tf_op jit(solution)/shard_map/ppermute | solution.py:188
  149.8 18.8 %collective-permute-start.33 = (bf16[64,2048]{1,0:T(8,128)(2,1)S(1)}, bf16[64,2048]{1,0:T(8,128)(2,1)S(1)}, u32[]{:S(2)}, u32[]{:S(2)}) collective-permute-start(bf16[64,2048]{1,0:T(8,128)(2,1)S(1)} %get-tuple-element.58), channel_id=1, source_target_pairs={{0,64},{64,128},{128,192},{192,0},{1,65},{65,129},{129,193},{193,1... | collective-permute-start | bytes 786440 | tf_op jit(solution)/shard_map/ppermute | solution.py:188
  150.4 18.1 %collective-permute-start.34 = (bf16[64,2048]{1,0:T(8,128)(2,1)S(1)}, bf16[64,2048]{1,0:T(8,128)(2,1)S(1)}, u32[]{:S(2)}, u32[]{:S(2)}) collective-permute-start(bf16[64,2048]{1,0:T(8,128)(2,1)S(1)} %get-tuple-element.59), channel_id=1, source_target_pairs={{0,128},{64,192},{128,0},{192,64},{1,129},{65,193},{129,1},{193,65... | collective-permute-start | bytes 786440 | tf_op jit(solution)/shard_map/ppermute | solution.py:188
  152.0 16.5 %collective-permute-start.35 = (bf16[64,2048]{1,0:T(8,128)(2,1)S(1)}, bf16[64,2048]{1,0:T(8,128)(2,1)S(1)}, u32[]{:S(2)}, u32[]{:S(2)}) collective-permute-start(bf16[64,2048]{1,0:T(8,128)(2,1)S(1)} %get-tuple-element.60), channel_id=1, source_target_pairs={{0,192},{64,0},{128,64},{192,128},{1,193},{65,1},{129,65},{193,129... | collective-permute-start | bytes 786440 | tf_op jit(solution)/shard_map/ppermute | solution.py:188
  169.5 22.7 %all-to-all-start.2 = ((bf16[16,8,2048]{2,1,0:T(8,128)(2,1)}), bf16[16,8,2048]{2,1,0:T(8,128)(2,1)S(1)}, u32[]{:S(2)}, u32[]{:S(2)}) async-start(bf16[16,8,2048]{2,1,0:T(8,128)(2,1)} %maximum_bitcast_fusion), calls=%async_computation.2 | async-start | bytes 1048576 | tf_op jit(solution)/shard_map/all_to_all | solution.py:290
  (27 other events, 279.4 us)
